TPU v7x, 32 devices: a whole 2x2x4 slice. The times are simulated.
32 devices in a mesh: wide: 8 (over z, x), narrow: 4 (over y, core).
Axes of the slice: x: 2, y: 2, z: 4, core: 2. Of those that a mesh axis runs over, the one named last changes fastest.
Arguments:
- block_in: bfloat16 [160, 200, 768], P(('wide', 'narrow')), may hold values from -6 to 6
- out_grad: bfloat16 [160, 200, 768], P(('wide', 'narrow')), may hold values from -6 to 6
- mim_mask: int32 [160, 200], P(('wide', 'narrow')), may hold values from 0 to 1, as said below
- rel_index: int32 [200, 200], replicated, may hold values from 0 to 731
- qkv_weight: bfloat16 [768, 2304], replicated, may hold values from -0.21875 to 0.21875
- proj_weight: bfloat16 [768, 768], replicated, may hold values from -0.875 to 0.875
- up_weight: bfloat16 [768, 3072], P(None, 'narrow'), may hold values from -0.21875 to 0.21875
- down_weight: bfloat16 [768, 3072], P(None, 'narrow'), may hold values from -0.109375 to 0.109375
- vectors: float32 [10, 768], replicated
- up_bias: float32 [3072], replicated, may hold values from -1.5 to 1.5
- rel_table: float32 [732, 12], replicated, may hold values from -4 to 4
- qkv_master: float32 [768, 2304], P('wide', 'narrow'), may hold values from -0.21875 to 0.21875
- qkv_mean: float32 [768, 2304], P('wide', 'narrow'), may hold values from -0.00061035156 to 0.00061035156
- qkv_square: float32 [768, 2304], P('wide', 'narrow'), may hold values from 7.064254e-11 to 1.1302806e-09
- proj_master: float32 [768, 768], P('wide', 'narrow'), may hold values from -0.875 to 0.875
- proj_mean: float32 [768, 768], P('wide', 'narrow'), may hold values from -0.00061035156 to 0.00061035156
- proj_square: float32 [768, 768], P('wide', 'narrow'), may hold values from 7.064254e-11 to 1.1302806e-09
- up_master: float32 [768, 3072], P('wide', 'narrow'), may hold values from -0.21875 to 0.21875
- up_mean: float32 [768, 3072], P('wide', 'narrow'), may hold values from -0.00061035156 to 0.00061035156
- up_square: float32 [768, 3072], P('wide', 'narrow'), may hold values from 7.064254e-11 to 1.1302806e-09
- down_master: float32 [768, 3072], P('wide', 'narrow'), may hold values from -0.109375 to 0.109375
- down_mean: float32 [768, 3072], P('wide', 'narrow'), may hold values from -0.00061035156 to 0.00061035156
- down_square: float32 [768, 3072], P('wide', 'narrow'), may hold values from 7.064254e-11 to 1.1302806e-09
- vector_mean: float32 [10, 768], replicated, may hold values from -0.001953125 to 0.001953125
- vector_square: float32 [10, 768], replicated, may hold values from 6.3578287e-10 to 1.0172526e-08
- bias_mean: float32 [3072], replicated, may hold values from -0.001953125 to 0.001953125
- bias_square: float32 [3072], replicated, may hold values from 4.2385526e-11 to 1.695421e-10
- table_mean: float32 [732, 12], replicated, may hold values from -0.001953125 to 0.001953125
- table_square: float32 [732, 12], replicated, may hold values from 4.2385526e-11 to 1.695421e-10
Outputs:
- block_out: bfloat16 [160, 200, 768], P(('wide', 'narrow'))
- input_grad: float32 [160, 200, 768], P(('wide', 'narrow'))
- grad_norm: float32 [], replicated
- qkv_mean_new: float32 [768, 2304], P('wide', 'narrow')
- qkv_square_new: float32 [768, 2304], P('wide', 'narrow')
- qkv_new: float32 [768, 2304], P('wide', 'narrow')
- qkv_copy: bfloat16 [768, 2304], P('wide', 'narrow')
- proj_mean_new: float32 [768, 768], P('wide', 'narrow')
- proj_square_new: float32 [768, 768], P('wide', 'narrow')
- proj_new: float32 [768, 768], P('wide', 'narrow')
- proj_copy: bfloat16 [768, 768], P('wide', 'narrow')
- up_mean_new: float32 [768, 3072], P('wide', 'narrow')
- up_square_new: float32 [768, 3072], P('wide', 'narrow')
- up_new: float32 [768, 3072], P('wide', 'narrow')
- up_copy: bfloat16 [768, 3072], P('wide', 'narrow')
- down_mean_new: float32 [768, 3072], P('wide', 'narrow')
- down_square_new: float32 [768, 3072], P('wide', 'narrow')
- down_new: float32 [768, 3072], P('wide', 'narrow')
- down_copy: bfloat16 [768, 3072], P('wide', 'narrow')
- vector_mean_new: float32 [10, 768], replicated
- vector_square_new: float32 [10, 768], replicated
- vectors_new: float32 [10, 768], replicated
- bias_mean_new: float32 [3072], replicated
- bias_square_new: float32 [3072], replicated
- up_bias_new: float32 [3072], replicated
- table_mean_new: float32 [732, 12], replicated
- table_square_new: float32 [732, 12], replicated
- table_new: float32 [732, 12], replicated
Inputs may be any that keep to these rules, and one draw needn't show every extreme that they name: `mim_mask`: each image masks its own share of patches, from almost none to about three quarters, very unequal between images; position 0 and positions from 197 on are never masked.
All inputs are finite; a program needn't handle non-finite values.
Results may differ from a plain program's by a relative error of at most 0.012.
Values may be sent and summed in bfloat16 or wider, within the bound.
No kernel may reach another device: no remote copies, remote signals or barrier semaphores. Data moves between devices by JAX's collectives and lax.ppermute only.
A program may use at most 192 MiB of HBM per device.

v0:
```python
import jax
import jax.numpy as jnp
from jax import lax
from jax.sharding import PartitionSpec as P

VALID = 197
STEP = 10
norm_eps = 1e-06
clip_eps = 1e-06
max_norm = 1.0
beta_one = 0.9
beta_two = 0.999
adam_eps = 1e-08
rate_matrix = 0.05
rate_small = 0.4
weight_decay = 0.05
exact_prec = lax.Precision.HIGHEST
contract_rows = (((0,), (0,)), ((), ()))
contract_cols = (((1,), (1,)), ((), ()))


def split_up(shard, dim, peers):
    shape = shard.shape
    parts = shard.reshape(*shape[:dim], peers, shape[dim] // peers, *shape[dim + 1 :])
    return jnp.moveaxis(parts, dim, 0)


def sent_and_summed(shard, axis, dim):
    parts = split_up(shard, dim, lax.axis_size(axis))
    arrived = lax.all_to_all(parts, axis, split_axis=0, concat_axis=0, tiled=True)
    return arrived.astype(jnp.float32).sum(axis=0)


def in_one_piece(arrays, axis, dim, along):
    ends, at = ([], 0)
    for a in arrays[:-1]:
        at += a.shape[along]
        ends.append(at)
    both = jnp.concatenate(arrays, axis=along)
    return tuple(jnp.split(sent_and_summed(both, axis, dim), ends, axis=along))


def layer_stats(values, gain_vec, shift_vec):
    center = values - jnp.mean(values, -1, keepdims=True)
    factor = lax.rsqrt(jnp.mean(center * center, -1, keepdims=True) + norm_eps)
    normed = center * factor
    return (normed * gain_vec + shift_vec, normed, factor)


def layer_back(grad, normed, factor, gain_vec):
    scaled = grad * gain_vec
    return factor * (
        scaled
        - jnp.mean(scaled, -1, keepdims=True)
        - normed * jnp.mean(scaled * normed, -1, keepdims=True)
    )


def gelu_exact(values):
    return 0.5 * values * (1.0 + jax.scipy.special.erf(values * 0.7071067811865476))


def gelu_slope(values):
    return (
        0.5 * (1.0 + jax.scipy.special.erf(values * 0.7071067811865476))
        + values * jnp.exp(-0.5 * values * values) * 0.3989422804014327
    )


def rel_bias(rel_index, rel_table):
    seq_len = rel_index.shape[0]
    table_rows, heads = rel_table.shape
    blocks = rel_index.reshape(8, seq_len // 8, seq_len)

    def one_block(index_rows):
        onehot = (
            index_rows[:, :, None] == jnp.arange(table_rows, dtype=jnp.int32)[None, None, :]
        ).astype(jnp.float32)
        return jnp.einsum("qkr,rh->hqk", onehot, rel_table, precision=exact_prec)

    pieces = lax.map(one_block, blocks)
    return jnp.transpose(pieces, (1, 0, 2, 3)).reshape(heads, seq_len, seq_len)


def table_grad(rel_index, grad_rel, table_rows):
    heads, seq_len = (grad_rel.shape[0], grad_rel.shape[1])
    index_blocks = rel_index.reshape(8, seq_len // 8, seq_len)
    grad_blocks = jnp.moveaxis(grad_rel.reshape(heads, 8, seq_len // 8, seq_len), 1, 0)

    def add_block(total, paired):
        index_rows, grad_rows = paired
        onehot = (
            index_rows[:, :, None] == jnp.arange(table_rows, dtype=jnp.int32)[None, None, :]
        ).astype(jnp.float32)
        return (total + jnp.einsum("qkr,hqk->rh", onehot, grad_rows, precision=exact_prec), None)

    total, unused = lax.scan(
        add_block, jnp.zeros((table_rows, heads), jnp.float32), (index_blocks, grad_blocks)
    )
    return total


def adam_update(master, mean, square, grad, rate, decay):
    mean_new = beta_one * mean + (1.0 - beta_one) * grad
    square_new = beta_two * square + (1.0 - beta_two) * grad * grad
    fix_one = 1.0 - beta_one**STEP
    fix_two = 1.0 - beta_two**STEP
    direction = mean_new / fix_one / (jnp.sqrt(square_new / fix_two) + adam_eps)
    return (mean_new, square_new, master - rate * (direction + decay * master))


def shards(
    block_in,
    out_grad,
    mim_mask,
    rel_index,
    qkv_weight,
    proj_weight,
    up_weight,
    down_weight,
    vectors,
    up_bias,
    rel_table,
    qkv_master,
    qkv_mean,
    qkv_square,
    proj_master,
    proj_mean,
    proj_square,
    up_master,
    up_mean,
    up_square,
    down_master,
    down_mean,
    down_square,
    vector_mean,
    vector_square,
    bias_mean,
    bias_square,
    table_mean,
    table_square,
):
    images, seq_len, width = block_in.shape
    table_rows, heads = rel_table.shape
    head_dim = width // heads
    token_rows = images * seq_len
    factor_scale = head_dim ** (-0.5)
    local_ff = up_weight.shape[1]
    offset = lax.axis_index("narrow") * local_ff
    inputs = block_in.reshape(token_rows, width).astype(jnp.float32)
    first_norm, hat_one, factor_one = layer_stats(inputs, vectors[4], vectors[5])
    first_b = first_norm.astype(jnp.bfloat16)
    qkv_bias = jnp.concatenate([vectors[0], jnp.zeros_like(vectors[0]), vectors[1]])
    qkv_b = (jnp.dot(first_b, qkv_weight, preferred_element_type=jnp.float32) + qkv_bias).astype(
        jnp.bfloat16
    )
    parts = qkv_b.reshape(images, seq_len, 3, heads, head_dim)
    query, keys, values = (parts[:, :, 0], parts[:, :, 1], parts[:, :, 2])
    bias_all = rel_bias(rel_index, rel_table)
    key_keep = (jnp.arange(seq_len) < VALID)[None, None, None, :]

    def score_block():
        raw = (
            jnp.einsum("bqhd,bkhd->bhqk", query, keys, preferred_element_type=jnp.float32)
            * factor_scale
            + bias_all[None]
        )
        return jnp.where(key_keep, raw, -1e30)

    scores = score_block()
    log_total = jax.nn.logsumexp(scores, -1, keepdims=True)
    probs_b = jnp.exp(scores - log_total).astype(jnp.bfloat16)
    mixed = jnp.einsum("bhqk,bkhd->bqhd", probs_b, values, preferred_element_type=jnp.float32)
    heads_b = mixed.reshape(token_rows, width).astype(jnp.bfloat16)
    attn = jnp.dot(heads_b, proj_weight, preferred_element_type=jnp.float32) + vectors[2]
    middle = inputs + vectors[8] * attn
    second_norm, hat_two, factor_two = layer_stats(middle, vectors[6], vectors[7])
    second_b = second_norm.astype(jnp.bfloat16)
    gathered = lax.all_gather(second_b, "narrow", axis=0, tiled=True)
    local_bias = lax.dynamic_slice_in_dim(up_bias, offset, local_ff)
    hidden_pre = jnp.dot(gathered, up_weight, preferred_element_type=jnp.float32) + local_bias
    active_b = gelu_exact(hidden_pre).astype(jnp.bfloat16)
    block_rows = active_b
    branch = lax.psum_scatter(
        lax.dot_general(
            block_rows, down_weight, contract_cols, preferred_element_type=jnp.float32
        ).astype(jnp.bfloat16),
        "narrow",
        scatter_dimension=0,
        tiled=True,
    ).astype(jnp.float32)
    mlp_out = branch + vectors[3]
    block_out = (middle + vectors[9] * mlp_out).astype(jnp.bfloat16).reshape(images, seq_len, width)
    cotangent = out_grad.reshape(token_rows, width).astype(jnp.float32) * mim_mask.reshape(
        token_rows, 1
    ).astype(jnp.float32)
    grad_scale_two = jnp.sum(cotangent * mlp_out, 0)
    down_in_b = (vectors[9] * cotangent).astype(jnp.bfloat16)
    grad_down_bias = jnp.sum(down_in_b, 0, dtype=jnp.float32)
    down_all = lax.all_gather(down_in_b, "narrow", axis=0, tiled=True)
    active_grad = jnp.dot(down_all, down_weight, preferred_element_type=jnp.float32)
    grad_down = lax.dot_general(
        down_all, active_b, contract_rows, preferred_element_type=jnp.float32
    )
    pre_grad_b = (active_grad * gelu_slope(hidden_pre)).astype(jnp.bfloat16)
    grad_up = lax.dot_general(
        gathered, pre_grad_b, contract_rows, preferred_element_type=jnp.float32
    )
    local_bias_grad = jnp.sum(pre_grad_b, 0, dtype=jnp.float32)
    grad_bias = lax.dynamic_update_slice_in_dim(
        jnp.zeros(up_bias.shape, jnp.float32), local_bias_grad, offset, 0
    )
    block_rows = pre_grad_b
    grad_second = lax.psum_scatter(
        lax.dot_general(block_rows, up_weight, contract_cols, preferred_element_type=jnp.float32),
        "narrow",
        scatter_dimension=0,
        tiled=True,
    )
    grad_gain_two = jnp.sum(grad_second * hat_two, 0)
    grad_shift_two = jnp.sum(grad_second, 0)
    grad_middle = cotangent + layer_back(grad_second, hat_two, factor_two, vectors[6])
    grad_scale_one = jnp.sum(grad_middle * attn, 0)
    proj_in_b = (vectors[8] * grad_middle).astype(jnp.bfloat16)
    grad_proj_bias = jnp.sum(proj_in_b, 0, dtype=jnp.float32)
    grad_proj = lax.dot_general(
        heads_b, proj_in_b, contract_rows, preferred_element_type=jnp.float32
    )
    heads_grad_b = lax.dot_general(
        proj_in_b, proj_weight, contract_cols, preferred_element_type=jnp.float32
    ).astype(jnp.bfloat16)
    out_heads = heads_grad_b.reshape(images, seq_len, heads, head_dim)
    probs = jnp.exp(score_block() - log_total)
    probs_b = probs.astype(jnp.bfloat16)
    grad_values = jnp.einsum(
        "bhqk,bqhd->bkhd", probs_b, out_heads, preferred_element_type=jnp.float32
    )
    grad_probs = jnp.einsum(
        "bqhd,bkhd->bhqk", out_heads, values, preferred_element_type=jnp.float32
    )
    row_total = jnp.sum(grad_probs * probs, -1, keepdims=True)
    grad_scores_b = (probs * (grad_probs - row_total)).astype(jnp.bfloat16)
    grad_query = (
        jnp.einsum("bhqk,bkhd->bqhd", grad_scores_b, keys, preferred_element_type=jnp.float32)
        * factor_scale
    )
    grad_keys = (
        jnp.einsum("bhqk,bqhd->bkhd", grad_scores_b, query, preferred_element_type=jnp.float32)
        * factor_scale
    )
    grad_rel = jnp.sum(grad_scores_b, 0, dtype=jnp.float32)
    grad_table = table_grad(rel_index, grad_rel, table_rows)
    grad_qkv_b = (
        jnp.stack([grad_query, grad_keys, grad_values], 2)
        .reshape(token_rows, 3 * width)
        .astype(jnp.bfloat16)
    )
    column_sums = jnp.sum(grad_qkv_b, 0, dtype=jnp.float32)
    grad_qkv = lax.dot_general(
        first_b, grad_qkv_b, contract_rows, preferred_element_type=jnp.float32
    )
    grad_first = lax.dot_general(
        grad_qkv_b, qkv_weight, contract_cols, preferred_element_type=jnp.float32
    )
    grad_gain_one = jnp.sum(grad_first * hat_one, 0)
    grad_shift_one = jnp.sum(grad_first, 0)
    input_grad = (grad_middle + layer_back(grad_first, hat_one, factor_one, vectors[4])).reshape(
        images, seq_len, width
    )
    grad_vectors = jnp.stack(
        [
            column_sums[:width],
            column_sums[2 * width :],
            grad_proj_bias,
            grad_down_bias,
            grad_gain_one,
            grad_shift_one,
            grad_gain_two,
            grad_shift_two,
            grad_scale_one,
            grad_scale_two,
        ]
    )
    grad_vectors, grad_bias, grad_table = lax.psum(
        (grad_vectors, grad_bias, grad_table), ("wide", "narrow")
    )
    qkv_part, proj_part = (
        lax.psum_scatter(
            grad_qkv.astype(jnp.bfloat16), "narrow", scatter_dimension=1, tiled=True
        ).astype(jnp.float32),
        lax.psum_scatter(
            grad_proj.astype(jnp.bfloat16), "narrow", scatter_dimension=1, tiled=True
        ).astype(jnp.float32),
    )
    up_part, down_part = (grad_up, grad_down)
    qkv_shard, proj_shard, up_shard, down_shard = in_one_piece(
        (
            qkv_part.astype(jnp.bfloat16),
            proj_part.astype(jnp.bfloat16),
            up_part.astype(jnp.bfloat16),
            down_part.astype(jnp.bfloat16),
        ),
        "wide",
        0,
        1,
    )
    shard_squares = (
        jnp.sum(qkv_shard * qkv_shard)
        + jnp.sum(proj_shard * proj_shard)
        + jnp.sum(up_shard * up_shard)
        + jnp.sum(down_shard * down_shard)
    )
    large_squares = lax.psum(shard_squares, ("wide", "narrow"))
    small_squares = (
        jnp.sum(grad_vectors * grad_vectors)
        + jnp.sum(grad_bias * grad_bias)
        + jnp.sum(grad_table * grad_table)
    )
    grad_norm = jnp.sqrt(large_squares + small_squares)
    clip = jnp.minimum(1.0, max_norm / (grad_norm + clip_eps))
    results = [block_out, input_grad, grad_norm]
    for master, mean, square, grad in (
        (qkv_master, qkv_mean, qkv_square, qkv_shard),
        (proj_master, proj_mean, proj_square, proj_shard),
        (up_master, up_mean, up_square, up_shard),
        (down_master, down_mean, down_square, down_shard),
    ):
        mean_new, square_new, master_new = adam_update(
            master, mean, square, clip * grad, rate_matrix, weight_decay
        )
        results += [mean_new, square_new, master_new, master_new.astype(jnp.bfloat16)]
    for master, mean, square, grad in (
        (vectors, vector_mean, vector_square, grad_vectors),
        (up_bias, bias_mean, bias_square, grad_bias),
        (rel_table, table_mean, table_square, grad_table),
    ):
        mean_new, square_new, master_new = adam_update(
            master, mean, square, clip * grad, rate_small, 0.0
        )
        results += [mean_new, square_new, master_new]
    return tuple(results)


def solution(mesh):
    in_specs = (
        P(("wide", "narrow"), None, None),
        P(("wide", "narrow"), None, None),
        P(("wide", "narrow"), None),
        P(),
        P(),
        P(),
        P(None, "narrow"),
        P(None, "narrow"),
        P(),
        P(),
        P(),
        P("wide", "narrow"),
        P("wide", "narrow"),
        P("wide", "narrow"),
        P("wide", "narrow"),
        P("wide", "narrow"),
        P("wide", "narrow"),
        P("wide", "narrow"),
        P("wide", "narrow"),
        P("wide", "narrow"),
        P("wide", "narrow"),
        P("wide", "narrow"),
        P("wide", "narrow"),
        P(),
        P(),
        P(),
        P(),
        P(),
        P(),
    )
    out_specs = (
        P(("wide", "narrow"), None, None),
        P(("wide", "narrow"), None, None),
        P(),
        P("wide", "narrow"),
        P("wide", "narrow"),
        P("wide", "narrow"),
        P("wide", "narrow"),
        P("wide", "narrow"),
        P("wide", "narrow"),
        P("wide", "narrow"),
        P("wide", "narrow"),
        P("wide", "narrow"),
        P("wide", "narrow"),
        P("wide", "narrow"),
        P("wide", "narrow"),
        P("wide", "narrow"),
        P("wide", "narrow"),
        P("wide", "narrow"),
        P("wide", "narrow"),
        P(),
        P(),
        P(),
        P(),
        P(),
        P(),
        P(),
        P(),
        P(),
    )
    return jax.shard_map(shards, mesh=mesh, in_specs=in_specs, out_specs=out_specs, check_vma=False)
```

profile of v0, /device:TPU:0, one launch (start us, length us, event | category | flops | bytes accessed | tf_op | source)
XLA Modules:
  0.0 806.3 jit_solution(16619423688516278176)
XLA Ops:
  17.9 79.3 %while.21 = (s32[]{:T(128)}, f32[8,12,25,200]{3,1,2,0:T(8,128)}, s32[8,25,200]{2,1,0:T(8,128)}, f32[732,12]{0,1:T(8,128)}, s32[]{:T(128)}) while((s32[]{:T(128)}, f32[8,12,25,200]{3,1,2,0:T(8,128)}, s32[8,25,200]{2,1,0:T(8,128)}, f32[732,12]{0,1:T(8,128)}, s32[]{:T(128)}) %tuple.94), condition=%wide.region_3.4_spmd, body=%wide.region_2.3_spmd.sunk | while | flops 530700000 | bytes 518829 | solution.py:81
  38.5 9.2 %fusion.86 = f32[8,12,25,200]{3,1,2,0:T(8,128)} fusion(f32[8,12,25,200]{3,1,2,0:T(8,128)} %get-tuple-element.246, s32[]{:T(128)S(6)} %copy.134, s32[25,200]{1,0:T(8,128)S(1)} %dynamic-slice_bitcast_fusion.4, f32[732,12]{0,1:T(8,128)} %get-tuple-element.253), kind=kOutput, calls=%fused_computation.4.clone.1 | convolution fusion | flops 530700000 | bytes 478756 | tf_op jit(solution)/shard_map/while/body/eval_jaxpr/qkr,rh->hqk/dot_general | solution.py:79
  58.3 9.1 %fusion.86 = f32[8,12,25,200]{3,1,2,0:T(8,128)} fusion(f32[8,12,25,200]{3,1,2,0:T(8,128)} %get-tuple-element.246, s32[]{:T(128)S(6)} %copy.134, s32[25,200]{1,0:T(8,128)S(1)} %dynamic-slice_bitcast_fusion.4, f32[732,12]{0,1:T(8,128)} %get-tuple-element.253), kind=kOutput, calls=%fused_computation.4.clone.1 | convolution fusion | flops 530700000 | bytes 478756 | tf_op jit(solution)/shard_map/while/body/eval_jaxpr/qkr,rh->hqk/dot_general | solution.py:79
  68.2 9.2 %fusion.86 = f32[8,12,25,200]{3,1,2,0:T(8,128)} fusion(f32[8,12,25,200]{3,1,2,0:T(8,128)} %get-tuple-element.246, s32[]{:T(128)S(6)} %copy.134, s32[25,200]{1,0:T(8,128)S(1)} %dynamic-slice_bitcast_fusion.4, f32[732,12]{0,1:T(8,128)} %get-tuple-element.253), kind=kOutput, calls=%fused_computation.4.clone.1 | convolution fusion | flops 530700000 | bytes 478756 | tf_op jit(solution)/shard_map/while/body/eval_jaxpr/qkr,rh->hqk/dot_general | solution.py:79
  78.1 9.2 %fusion.86 = f32[8,12,25,200]{3,1,2,0:T(8,128)} fusion(f32[8,12,25,200]{3,1,2,0:T(8,128)} %get-tuple-element.246, s32[]{:T(128)S(6)} %copy.134, s32[25,200]{1,0:T(8,128)S(1)} %dynamic-slice_bitcast_fusion.4, f32[732,12]{0,1:T(8,128)} %get-tuple-element.253), kind=kOutput, calls=%fused_computation.4.clone.1 | convolution fusion | flops 530700000 | bytes 478756 | tf_op jit(solution)/shard_map/while/body/eval_jaxpr/qkr,rh->hqk/dot_general | solution.py:79
  88.0 9.2 %fusion.86 = f32[8,12,25,200]{3,1,2,0:T(8,128)} fusion(f32[8,12,25,200]{3,1,2,0:T(8,128)} %get-tuple-element.246, s32[]{:T(128)S(6)} %copy.134, s32[25,200]{1,0:T(8,128)S(1)} %dynamic-slice_bitcast_fusion.4, f32[732,12]{0,1:T(8,128)} %get-tuple-element.253), kind=kOutput, calls=%fused_computation.4.clone.1 | convolution fusion | flops 530700000 | bytes 478756 | tf_op jit(solution)/shard_map/while/body/eval_jaxpr/qkr,rh->hqk/dot_general | solution.py:79
  110.7 14.9 %reshape.239 = bf16[5,200,3,12,64]{4,3,2,1,0:T(8,128)(2,1)} reshape(bf16[1000,2304]{1,0:T(8,128)(2,1)} %add_convert_fusion) | data formatting | bytes 9216000 | tf_op jit(solution)/shard_map/reshape | solution.py:157
  195.1 41.3 %all-gather.3.cloned.1.call-done = bf16[4000,768]{1,0:T(8,128)(2,1)} async-done(((bf16[1000,768]{1,0:T(8,128)(2,1)}), bf16[4000,768]{1,0:T(8,128)(2,1)}) %all-gather.3.cloned.1.call-update) | async-done | bytes 6144016 | tf_op jit(solution)/shard_map/all_gather | solution.py:179
  236.4 12.7 %multiply_convert_fusion.1 = (bf16[4000,768]{1,0:T(8,128)(2,1)}, f32[4000,768]{1,0:T(8,128)}) fusion(f32[768]{0:T(1024)} %dynamic_slice.14, bf16[4000,768]{1,0:T(8,128)(2,1)} %all-gather.3.cloned.1.call-done, bf16[768,768]{1,0:T(8,128)(2,1)} %param.39), kind=kOutput, calls=%fused_computation.26 | convolution fusion | flops 4737024000 | bytes 25758720 | tf_op jit(solution)/shard_map/dot_general | solution.py:181
  249.0 34.4 %all-gather.5.cloned.1.call-done = bf16[4000,768]{1,0:T(8,128)(2,1)} async-done(((bf16[1000,768]{1,0:T(8,128)(2,1)}), bf16[4000,768]{1,0:T(8,128)(2,1)}) %all-gather.5.cloned.1.call-update) | async-done | bytes 6144016 | tf_op jit(solution)/shard_map/all_gather | solution.py:200
  283.5 12.4 %convert_reduce_fusion.1 = (f32[768]{0:T(1024)}, bf16[4000,768]{1,0:T(8,128)(2,1)S(1)}) fusion(f32[4000,768]{1,0:T(8,128)} %get-tuple-element.182, f32[768]{0:T(1024)} %dynamic_slice.14, bf16[4000,768]{1,0:T(8,128)(2,1)} %all-gather.5.cloned.1.call-done, bf16[768,768]{1,0:T(8,128)(2,1)} %param.40), kind=kOutput, calls=%fused_computation.23 | convolution fusion | flops 4758526976 | bytes 25761792 | tf_op jit(solution)/shard_map/dot_general | solution.py:201
  306.8 12.6 %convolution_convert_fusion = bf16[4000,768]{1,0:T(8,128)(2,1)} fusion(bf16[4000,768]{1,0:T(8,128)(2,1)} %get-tuple-element.181, bf16[768,768]{1,0:T(8,128)(2,1)} %param.40), kind=kOutput, calls=%fused_computation.36 | convolution fusion | flops 4721664000 | bytes 13467648 | tf_op jit(solution)/shard_map/dot_general | solution.py:185
  323.2 81.1 %reduce-scatter.7.cloned.1.call-done = f32[1000,768]{1,0:T(8,128)} async-done(((f32[4000,768]{1,0:T(8,128)}), f32[1000,768]{1,0:T(8,128)}) %reduce-scatter.7.cloned.1.call-update) | async-done | bytes 3072016 | tf_op jit(solution)/shard_map/reduce_scatter | solution.py:214
  409.2 55.5 %reduce-scatter.5.cloned.1.call-done = bf16[1000,768]{1,0:T(8,128)(2,1)} async-done(((bf16[4000,768]{1,0:T(8,128)(2,1)}), bf16[1000,768]{1,0:T(8,128)(2,1)}) %reduce-scatter.5.cloned.1.call-update) | async-done | bytes 1536016 | tf_op jit(solution)/shard_map/reduce_scatter | solution.py:184
  496.0 13.1 %multiply_reduce_fusion = (f32[5,12,200]{2,1,0:T(8,128)S(1)}, f32[5,12,200,200]{2,3,1,0:T(8,128)}) fusion(f32[5,12,200,200]{2,3,1,0:T(8,128)} %copy-done.1, f32[5,12,200]{2,1,0:T(8,128)} %copy-done.9, bf16[5,200,12,64]{1,3,2,0:T(8,128)(2,1)} %copy.106, bf16[5,200,1,12,64]{1,4,3,0,2:T(8,128)(2,1)} %copy.124), kind=kOutput, calls=%fused_computation.25 | convolution fusion | flops 314388000 | bytes 22368000 | tf_op jit(solution)/shard_map/bqhd,bkhd->bhqk/dot_general | solution.py:238
  509.1 12.1 %convert_reduce_fusion = (f32[12,200,200]{1,2,0:T(8,128)}, bf16[5,12,200,200]{2,3,1,0:T(8,128)(2,1)S(1)}) fusion(f32[5,12,200,200]{2,3,1,0:T(8,128)} %get-tuple-element.184, f32[5,12,200]{2,1,0:T(8,128)S(1)} %get-tuple-element.183, f32[5,12,200,200]{2,3,1,0:T(8,128)} %copy-done.1, f32[5,12,200]{2,1,0:T(8,128)S(1)} %copy-done.10), kind=kLoop, calls=%fused_computation.22 | loop fusion | flops 13920000 | bytes 26016000 | tf_op jit(solution)/shard_map/reduce_sum | solution.py:251
  540.7 11.3 %copy.111 = bf16[5,200,3,12,64]{1,0,4,3,2:T(8,128)(2,1)} copy(bf16[5,200,3,12,64]{1,4,3,0,2:T(8,128)(2,1)} %get-tuple-element.165) | data formatting | bytes 9216000 | tf_op jit(solution)/shard_map/convert_element_type | solution.py:256
  552.0 13.8 %convert_element_type.177 = bf16[1000,2304]{0,1:T(8,128)(2,1)} reshape(bf16[5,200,3,12,64]{1,0,4,3,2:T(8,128)(2,1)} %copy.111) | data formatting | bytes 9216000 | tf_op jit(solution)/shard_map/convert_element_type | solution.py:256
  574.2 9.8 %convolution_convert_fusion.3 = bf16[768,768]{0,1:T(8,128)(2,1)} fusion(bf16[4000,768]{1,0:T(8,128)(2,1)} %all-gather.5.cloned.1.call-done, bf16[4000,768]{1,0:T(8,128)(2,1)} %get-tuple-element.181), kind=kOutput, calls=%fused_computation.79 | convolution fusion | flops 4719181824 | bytes 13467648 | tf_op jit(solution)/shard_map/dot_general | solution.py:202
  584.0 10.0 %convolution_convert_fusion.4 = bf16[768,768]{0,1:T(8,128)(2,1)} fusion(bf16[4000,768]{1,0:T(8,128)(2,1)} %all-gather.3.cloned.1.call-done, bf16[4000,768]{1,0:T(8,128)(2,1)} %copy-done.35), kind=kOutput, calls=%fused_computation.80 | convolution fusion | flops 4719181824 | bytes 13467648 | tf_op jit(solution)/shard_map/dot_general | solution.py:206
  594.1 20.7 %reduce-scatter.9.cloned.1.call-done = bf16[768,576]{0,1:T(8,128)(2,1)} async-done(((bf16[768,2304]{0,1:T(8,128)(2,1)}), bf16[768,576]{0,1:T(8,128)(2,1)}) %reduce-scatter.9.cloned.1.call-update) | async-done | bytes 884752 | tf_op jit(solution)/shard_map/reduce_scatter | solution.py:288
  650.4 10.1 %multiply_reduce_fusion.4 = (f32[768]{0:T(1024)S(1)}, f32[1000]{0:T(1024)}, f32[1000]{0:T(1024)}, f32[768]{0:T(1024)S(1)}, f32[1000,768]{1,0:T(8,128)}) fusion(f32[1000]{0:T(1024)} %rsqrt.21, f32[1000]{0:T(1024)} %div.123, bf16[5,200,768]{2,1,0:T(8,128)(2,1)} %param.33, f32[768]{0:T(1024)S(1)} %copy-done.27, bf16[1000,2304]{0,1:T(8,128)(2,1)} %convert_element_type.177, ...), kind=kOutput, calls=%fused_computation.45 | convolution fusion | flops 3548924416 | bytes 14316160 | tf_op jit(solution)/shard_map/dot_general | solution.py:262
  671.8 60.1 %while.22 = (s32[]{:T(128)}, f32[732,12]{0,1:T(8,128)}, s32[8,25,200]{2,1,0:T(8,128)}, f32[8,12,25,200]{3,2,0,1:T(8,128)}, s32[]{:T(128)}, /*index=5*/s32[]{:T(128)}) while((s32[]{:T(128)}, f32[732,12]{0,1:T(8,128)}, s32[8,25,200]{2,1,0:T(8,128)}, f32[8,12,25,200]{3,2,0,1:T(8,128)}, s32[]{:T(128)}, /*index=5*/s32[]{:T(128)}) %tuple.113), condition=%wide.region_39.40_spmd.clone, body=%wide.region_38.39_spmd.clone.sunk | while | flops 530717568 | bytes 850367 | solution.py:97
  739.2 41.4 %all-reduce.2 = (f32[]{:T(128)}, f32[10,768]{1,0:T(8,128)}, f32[3072]{0:T(1024)}, f32[732,12]{0,1:T(8,128)}) all-reduce(f32[]{:T(128)S(6)} %add.302, f32[10,768]{1,0:T(8,128)} %stack.59, f32[3072]{0:T(1024)S(1)} %dynamic_update_slice.7, f32[732,12]{0,1:T(8,128)} %get-tuple-element.73), channel_id=1, replica_groups=mesh['wide'=8,'narrow'=4] {'wide','narrow'}, use_global_device_ids=true, to_apply=%region_22.23 | all-reduce | flops 19537 | bytes 156296 | tf_op jit(solution)/shard_map/psum | solution.py:313
  (215 shorter events, 331.6 us)
Async XLA Ops:
  7.2 95.4 %copy-start = (bf16[768,2304]{1,0:T(8,128)(2,1)S(1)}, bf16[768,2304]{1,0:T(8,128)(2,1)}, u32[]{:S(2)}) copy-start(bf16[768,2304]{1,0:T(8,128)(2,1)} %param.37) | copy-start | bytes 10616836
  7.2 229.1 %all-gather.3.cloned.1.call-start = ((), (), s32[]{:S(2)}) async-start(), calls=%async_computation.5 | async-start | bytes 7680000 | tf_op jit(solution)/shard_map/all_gather | solution.py:179
  188.0 95.5 %all-gather.5.cloned.1.call-start = ((), (), s32[]{:S(2)}) async-start(), calls=%async_computation.7 | async-start | bytes 7680000 | tf_op jit(solution)/shard_map/all_gather | solution.py:200
  193.6 210.7 %reduce-scatter.7.cloned.1.call-start = ((), (), s32[]{:S(2)}) async-start(), calls=%async_computation.8 | async-start | bytes 15360000 | tf_op jit(solution)/shard_map/reduce_scatter | solution.py:214
  283.5 15.1 %copy-start.34 = (bf16[768,768]{1,0:T(8,128)(2,1)S(1)}, bf16[768,768]{1,0:T(8,128)(2,1)}, u32[]{:S(2)}) copy-start(bf16[768,768]{1,0:T(8,128)(2,1)} %param.39) | copy-start | bytes 3538948
  306.5 158.1 %reduce-scatter.5.cloned.1.call-start = ((), (), s32[]{:S(2)}) async-start(), calls=%async_computation.6 | async-start | bytes 7680000 | tf_op jit(solution)/shard_map/reduce_scatter | solution.py:184
  319.4 274.7 %reduce-scatter.11.cloned.1.call-start = ((), (), s32[]{:S(2)}) async-start(), calls=%async_computation.10 | async-start | bytes 1474560 | tf_op jit(solution)/shard_map/reduce_scatter | solution.py:291
  323.2 141.5 %copy-start.23 = (f32[768]{0:T(1024)S(1)}, f32[768]{0:T(1024)}, u32[]{:S(2)}) copy-start(f32[768]{0:T(1024)} %get-tuple-element.105) | copy-start | bytes 9220
  323.2 141.5 %copy-start.25 = (f32[1000]{0:T(1024)S(1)}, f32[1000]{0:T(1024)}, u32[]{:S(2)}) copy-start(f32[1000]{0:T(1024)} %copy-done.24) | copy-start | bytes 12004
  464.6 10.0 %copy-start.30 = (f32[768]{0:T(1024)S(1)}, f32[768]{0:T(1024)}, u32[]{:S(2)}) copy-start(f32[768]{0:T(1024)} %get-tuple-element.111) | copy-start | bytes 9220
  483.7 131.0 %reduce-scatter.9.cloned.1.call-start = ((), (), s32[]{:S(2)}) async-start(), calls=%async_computation.9 | async-start | bytes 4423680 | tf_op jit(solution)/shard_map/reduce_scatter | solution.py:288
  496.0 13.1 %copy-start.10 = (f32[5,12,200]{2,1,0:T(8,128)S(1)}, f32[5,12,200]{2,1,0:T(8,128)}, u32[]{:S(2)}) copy-start(f32[5,12,200]{2,1,0:T(8,128)} %copy-done.9) | copy-start | bytes 144004
  509.1 19.9 %slice-start = ((s8[12288000]{0:T(1024)(128)(4,1)}), s8[4194304]{0:T(1024)(128)(4,1)S(1)}, s32[]{:S(2)}) async-start(s8[12288000]{0:T(1024)(128)(4,1)} %bitcast.122), calls=%async_computation.11 | async-start | bytes 8388608
  509.1 19.9 %slice-start.1 = ((s8[12288000]{0:T(1024)(128)(4,1)}), s8[4194304]{0:T(1024)(128)(4,1)S(1)}, s32[]{:S(2)}) async-start(s8[12288000]{0:T(1024)(128)(4,1)} %bitcast.122), calls=%async_computation.12 | async-start | bytes 8388608
  521.2 7.8 slice-start.2
  624.0 107.8 %all-to-all-start = ((bf16[8,96,2304]{2,1,0:T(8,128)(2,1)}), bf16[8,96,2304]{2,1,0:T(8,128)(2,1)}, u32[]{:S(2)}, u32[]{:S(2)}) async-start(bf16[8,96,2304]{2,1,0:T(8,128)(2,1)} %bitcast.126), calls=%async_computation.4 | async-start | bytes 7077888 | tf_op jit(solution)/shard_map/all_to_all | solution.py:30
  642.8 7.6 copy-start.27
  787.4 8.9 %copy-start.7 = (f32[96,2304]{1,0:T(8,128)S(1)}, f32[96,2304]{1,0:T(8,128)}, u32[]{:S(2)}) copy-start(f32[96,2304]{1,0:T(8,128)} %copy-done.6) | copy-start | bytes 2654212
  787.4 8.9 %copy-start.13 = (f32[96,768]{1,0:T(8,128)S(1)}, f32[96,768]{1,0:T(8,128)}, u32[]{:S(2)}) copy-start(f32[96,768]{1,0:T(8,128)} %param.53) | copy-start | bytes 884740
  787.4 8.9 %copy-start.14 = (f32[96,768]{1,0:T(8,128)S(1)}, f32[96,768]{1,0:T(8,128)}, u32[]{:S(2)}) copy-start(f32[96,768]{1,0:T(8,128)} %param.55) | copy-start | bytes 884740
  787.5 8.9 %copy-start.15 = (f32[96,768]{1,0:T(8,128)S(1)}, f32[96,768]{1,0:T(8,128)}, u32[]{:S(2)}) copy-start(f32[96,768]{1,0:T(8,128)} %param.54) | copy-start | bytes 884740
  787.5 8.9 %copy-start.16 = (f32[96,768]{1,0:T(8,128)S(1)}, f32[96,768]{1,0:T(8,128)}, u32[]{:S(2)}) copy-start(f32[96,768]{1,0:T(8,128)} %param.50) | copy-start | bytes 884740
  787.5 8.9 %copy-start.17 = (f32[96,768]{1,0:T(8,128)S(1)}, f32[96,768]{1,0:T(8,128)}, u32[]{:S(2)}) copy-start(f32[96,768]{1,0:T(8,128)} %param.52) | copy-start | bytes 884740
  787.5 8.9 %copy-start.18 = (f32[96,768]{1,0:T(8,128)S(1)}, f32[96,768]{1,0:T(8,128)}, u32[]{:S(2)}) copy-start(f32[96,768]{1,0:T(8,128)} %param.51) | copy-start | bytes 884740
  (22 other events, 86.5 us)
Sparse Core Ops, SparseCore 0:
  188.1 48.2 all-gather.2
  237.9 45.5 all-gather.4
  306.6 97.6 reduce-scatter.6
  406.7 57.8 reduce-scatter.4
  483.8 25.5 reduce-scatter.10
  574.3 40.3 reduce-scatter.8
where the time goes:
time: 818 us; the launch traced here: 806 us
  matrix products  258 us (32%)
  waiting for transfers between devices  233 us (28%)
  local copies, waits for them, and re-layouts  157 us (19%)
  other arithmetic  88.3 us (11%)
  blocking collectives  41.4 us (5%)
  between operations  21.4 us (3%)
    reduce_scatter x1, waiting for transfers between devices, shards(): lax.psum_scatter(lax.dot_general(block_rows, up_weight, contract_cols, pr...  81.1 us
    dot_general x8, matrix products, one_block(): return jnp.einsum('qkr,rh->hqk', onehot, rel_table, precision=exact_prec)  73.2 us
    reduce_scatter x1, waiting for transfers between devices, shards(): lax.psum_scatter(lax.dot_general(block_rows, down_weight, contract_cols,...  55.5 us
    dot_general x8, matrix products, add_block(): jnp.einsum('qkr,hqk->rh', onehot, grad_rows, precision=exact_prec)  45.6 us
    psum x1, blocking collectives, shards(): large_squares = lax.psum(shard_squares, ('wide', 'narrow'))  41.4 us
    all_gather x1, waiting for transfers between devices, shards(): gathered = lax.all_gather(second_b, 'narrow', axis=0, tiled=True)  41.3 us
    all_gather x1, waiting for transfers between devices, shards(): down_all = lax.all_gather(down_in_b, 'narrow', axis=0, tiled=True)  34.4 us
    unnamed x81, local copies, waits for them, and re-layouts  26.3 us
  transfers between devices with their start and end apart: 7, of which 5 were waited for; matrix products, arithmetic and copies ran while one was open for 31% of the time, Pallas kernels for 0%

commit v1 on v0

--- a/solution.py
+++ b/solution.py
@@ -310,7 +310,7 @@
         + jnp.sum(up_shard * up_shard)
         + jnp.sum(down_shard * down_shard)
     )
-    large_squares = lax.psum(shard_squares, ("wide", "narrow"))
+    large_squares = jnp.sum(lax.all_gather(shard_squares, ("wide", "narrow")), axis=0)
     small_squares = (
         jnp.sum(grad_vectors * grad_vectors)
         + jnp.sum(grad_bias * grad_bias)

time: 818 us -> 897 us (1.097)
  waiting for transfers between devices: 233 us -> 351 us
  blocking collectives: 41.4 us -> 0 us
    unnamed x6 -> x8, waiting for transfers between devices: 0.1 us -> 119 us
    psum x1 -> x0, blocking collectives: 41.4 us -> none  [shards(): large_squares = lax.psum(shard_squares, ('wide', 'narrow'))]
    unnamed x81 -> x89, local copies, waits for them, and re-layouts: 26.3 us -> 27.1 us
  transfers between devices with their start and end apart: 7 -> 8, of which waited for: 5 -> 6; matrix products, arithmetic and copies ran while one was open for 31% -> 29% of each run, Pallas kernels for 0% -> 0%
where the time goes in v1:
time: 897 us; the launch traced here: 885 us
  waiting for transfers between devices  351 us (39%)
  matrix products  259 us (29%)
  local copies, waits for them, and re-layouts  156 us (17%)
  other arithmetic  90.7 us (10%)
  between operations  21.2 us (2%)
    unnamed x8, waiting for transfers between devices  119 us
    reduce_scatter x1, waiting for transfers between devices, shards(): lax.psum_scatter(lax.dot_general(block_rows, up_weight, contract_cols, pr...  80.8 us
    dot_general x8, matrix products, one_block(): return jnp.einsum('qkr,rh->hqk', onehot, rel_table, precision=exact_prec)  73.2 us
    reduce_scatter x1, waiting for transfers between devices, shards(): lax.psum_scatter(lax.dot_general(block_rows, down_weight, contract_cols,...  55.5 us
    dot_general x8, matrix products, add_block(): jnp.einsum('qkr,hqk->rh', onehot, grad_rows, precision=exact_prec)  45.6 us
    all_gather x1, waiting for transfers between devices, shards(): gathered = lax.all_gather(second_b, 'narrow', axis=0, tiled=True)  41.3 us
    all_gather x1, waiting for transfers between devices, shards(): down_all = lax.all_gather(down_in_b, 'narrow', axis=0, tiled=True)  34.4 us
    unnamed x89, local copies, waits for them, and re-layouts  27.1 us
  transfers between devices with their start and end apart: 8, of which 6 were waited for; matrix products, arithmetic and copies ran while one was open for 29% of the time, Pallas kernels for 0%

profile of v1, /device:TPU:0, one launch (start us, length us, event | category | flops | bytes accessed | tf_op | source)
XLA Modules:
  0.0 884.6 jit_solution(10924581168113825059)
XLA Ops:
  17.9 79.3 %while.21 = (s32[]{:T(128)}, f32[8,12,25,200]{3,1,2,0:T(8,128)}, s32[8,25,200]{2,1,0:T(8,128)}, f32[732,12]{0,1:T(8,128)}, s32[]{:T(128)}) while((s32[]{:T(128)}, f32[8,12,25,200]{3,1,2,0:T(8,128)}, s32[8,25,200]{2,1,0:T(8,128)}, f32[732,12]{0,1:T(8,128)}, s32[]{:T(128)}) %tuple.94), condition=%wide.region_3.4_spmd, body=%wide.region_2.3_spmd.sunk | while | flops 530700000 | bytes 518829 | solution.py:81
  38.5 9.2 %fusion.86 = f32[8,12,25,200]{3,1,2,0:T(8,128)} fusion(f32[8,12,25,200]{3,1,2,0:T(8,128)} %get-tuple-element.246, s32[]{:T(128)S(6)} %copy.134, s32[25,200]{1,0:T(8,128)S(1)} %dynamic-slice_bitcast_fusion.4, f32[732,12]{0,1:T(8,128)} %get-tuple-element.253), kind=kOutput, calls=%fused_computation.4.clone.1 | convolution fusion | flops 530700000 | bytes 478756 | tf_op jit(solution)/shard_map/while/body/eval_jaxpr/qkr,rh->hqk/dot_general | solution.py:79
  58.3 9.1 %fusion.86 = f32[8,12,25,200]{3,1,2,0:T(8,128)} fusion(f32[8,12,25,200]{3,1,2,0:T(8,128)} %get-tuple-element.246, s32[]{:T(128)S(6)} %copy.134, s32[25,200]{1,0:T(8,128)S(1)} %dynamic-slice_bitcast_fusion.4, f32[732,12]{0,1:T(8,128)} %get-tuple-element.253), kind=kOutput, calls=%fused_computation.4.clone.1 | convolution fusion | flops 530700000 | bytes 478756 | tf_op jit(solution)/shard_map/while/body/eval_jaxpr/qkr,rh->hqk/dot_general | solution.py:79
  68.2 9.2 %fusion.86 = f32[8,12,25,200]{3,1,2,0:T(8,128)} fusion(f32[8,12,25,200]{3,1,2,0:T(8,128)} %get-tuple-element.246, s32[]{:T(128)S(6)} %copy.134, s32[25,200]{1,0:T(8,128)S(1)} %dynamic-slice_bitcast_fusion.4, f32[732,12]{0,1:T(8,128)} %get-tuple-element.253), kind=kOutput, calls=%fused_computation.4.clone.1 | convolution fusion | flops 530700000 | bytes 478756 | tf_op jit(solution)/shard_map/while/body/eval_jaxpr/qkr,rh->hqk/dot_general | solution.py:79
  78.1 9.2 %fusion.86 = f32[8,12,25,200]{3,1,2,0:T(8,128)} fusion(f32[8,12,25,200]{3,1,2,0:T(8,128)} %get-tuple-element.246, s32[]{:T(128)S(6)} %copy.134, s32[25,200]{1,0:T(8,128)S(1)} %dynamic-slice_bitcast_fusion.4, f32[732,12]{0,1:T(8,128)} %get-tuple-element.253), kind=kOutput, calls=%fused_computation.4.clone.1 | convolution fusion | flops 530700000 | bytes 478756 | tf_op jit(solution)/shard_map/while/body/eval_jaxpr/qkr,rh->hqk/dot_general | solution.py:79
  88.0 9.2 %fusion.86 = f32[8,12,25,200]{3,1,2,0:T(8,128)} fusion(f32[8,12,25,200]{3,1,2,0:T(8,128)} %get-tuple-element.246, s32[]{:T(128)S(6)} %copy.134, s32[25,200]{1,0:T(8,128)S(1)} %dynamic-slice_bitcast_fusion.4, f32[732,12]{0,1:T(8,128)} %get-tuple-element.253), kind=kOutput, calls=%fused_computation.4.clone.1 | convolution fusion | flops 530700000 | bytes 478756 | tf_op jit(solution)/shard_map/while/body/eval_jaxpr/qkr,rh->hqk/dot_general | solution.py:79
  110.7 14.9 %reshape.241 = bf16[5,200,3,12,64]{4,3,2,1,0:T(8,128)(2,1)} reshape(bf16[1000,2304]{1,0:T(8,128)(2,1)} %add_convert_fusion) | data formatting | bytes 9216000 | tf_op jit(solution)/shard_map/reshape | solution.py:157
  194.8 41.3 %all-gather.3.cloned.1.call-done = bf16[4000,768]{1,0:T(8,128)(2,1)} async-done(((bf16[1000,768]{1,0:T(8,128)(2,1)}), bf16[4000,768]{1,0:T(8,128)(2,1)}) %all-gather.3.cloned.1.call-update) | async-done | bytes 6144016 | tf_op jit(solution)/shard_map/all_gather | solution.py:179
  236.1 12.7 %multiply_convert_fusion.1 = (bf16[4000,768]{1,0:T(8,128)(2,1)}, f32[4000,768]{1,0:T(8,128)}) fusion(f32[768]{0:T(1024)} %dynamic_slice.14, bf16[4000,768]{1,0:T(8,128)(2,1)} %all-gather.3.cloned.1.call-done, bf16[768,768]{1,0:T(8,128)(2,1)} %param.39), kind=kOutput, calls=%fused_computation.26 | convolution fusion | flops 4737024000 | bytes 25758720 | tf_op jit(solution)/shard_map/dot_general | solution.py:181
  248.8 34.4 %all-gather.5.cloned.1.call-done = bf16[4000,768]{1,0:T(8,128)(2,1)} async-done(((bf16[1000,768]{1,0:T(8,128)(2,1)}), bf16[4000,768]{1,0:T(8,128)(2,1)}) %all-gather.5.cloned.1.call-update) | async-done | bytes 6144016 | tf_op jit(solution)/shard_map/all_gather | solution.py:200
  283.2 12.4 %convert_reduce_fusion.1 = (f32[768]{0:T(1024)}, bf16[4000,768]{1,0:T(8,128)(2,1)S(1)}) fusion(f32[4000,768]{1,0:T(8,128)} %get-tuple-element.182, f32[768]{0:T(1024)} %dynamic_slice.14, bf16[4000,768]{1,0:T(8,128)(2,1)} %all-gather.5.cloned.1.call-done, bf16[768,768]{1,0:T(8,128)(2,1)} %param.40), kind=kOutput, calls=%fused_computation.23 | convolution fusion | flops 4758526976 | bytes 25761792 | tf_op jit(solution)/shard_map/dot_general | solution.py:201
  306.7 12.7 %convolution_convert_fusion = bf16[4000,768]{1,0:T(8,128)(2,1)} fusion(bf16[4000,768]{1,0:T(8,128)(2,1)} %get-tuple-element.181, bf16[768,768]{1,0:T(8,128)(2,1)} %param.40), kind=kOutput, calls=%fused_computation.36 | convolution fusion | flops 4721664000 | bytes 13467648 | tf_op jit(solution)/shard_map/dot_general | solution.py:185
  323.3 80.8 %reduce-scatter.7.cloned.1.call-done = f32[1000,768]{1,0:T(8,128)} async-done(((f32[4000,768]{1,0:T(8,128)}), f32[1000,768]{1,0:T(8,128)}) %reduce-scatter.7.cloned.1.call-update) | async-done | bytes 3072016 | tf_op jit(solution)/shard_map/reduce_scatter | solution.py:214
  408.9 55.5 %reduce-scatter.5.cloned.1.call-done = bf16[1000,768]{1,0:T(8,128)(2,1)} async-done(((bf16[4000,768]{1,0:T(8,128)(2,1)}), bf16[1000,768]{1,0:T(8,128)(2,1)}) %reduce-scatter.5.cloned.1.call-update) | async-done | bytes 1536016 | tf_op jit(solution)/shard_map/reduce_scatter | solution.py:184
  495.5 13.1 %multiply_reduce_fusion = (f32[5,12,200]{2,1,0:T(8,128)S(1)}, f32[5,12,200,200]{2,3,1,0:T(8,128)}) fusion(f32[5,12,200,200]{2,3,1,0:T(8,128)} %copy-done.1, f32[5,12,200]{2,1,0:T(8,128)} %copy-done.9, bf16[5,200,12,64]{1,3,2,0:T(8,128)(2,1)} %copy.106, bf16[5,200,1,12,64]{1,4,3,0,2:T(8,128)(2,1)} %copy.124), kind=kOutput, calls=%fused_computation.25 | convolution fusion | flops 314388000 | bytes 22368000 | tf_op jit(solution)/shard_map/bqhd,bkhd->bhqk/dot_general | solution.py:238
  508.6 12.1 %convert_reduce_fusion = (f32[12,200,200]{1,2,0:T(8,128)}, bf16[5,12,200,200]{2,3,1,0:T(8,128)(2,1)S(1)}) fusion(f32[5,12,200,200]{2,3,1,0:T(8,128)} %get-tuple-element.184, f32[5,12,200]{2,1,0:T(8,128)S(1)} %get-tuple-element.183, f32[5,12,200,200]{2,3,1,0:T(8,128)} %copy-done.1, f32[5,12,200]{2,1,0:T(8,128)S(1)} %copy-done.10), kind=kLoop, calls=%fused_computation.22 | loop fusion | flops 13920000 | bytes 26016000 | tf_op jit(solution)/shard_map/reduce_sum | solution.py:251
  540.3 11.3 %copy.111 = bf16[5,200,3,12,64]{1,0,4,3,2:T(8,128)(2,1)} copy(bf16[5,200,3,12,64]{1,4,3,0,2:T(8,128)(2,1)} %get-tuple-element.165) | data formatting | bytes 9216000 | tf_op jit(solution)/shard_map/convert_element_type | solution.py:256
  551.6 13.8 %convert_element_type.177 = bf16[1000,2304]{0,1:T(8,128)(2,1)} reshape(bf16[5,200,3,12,64]{1,0,4,3,2:T(8,128)(2,1)} %copy.111) | data formatting | bytes 9216000 | tf_op jit(solution)/shard_map/convert_element_type | solution.py:256
  573.8 10.2 %convolution_convert_fusion.3 = bf16[768,768]{0,1:T(8,128)(2,1)} fusion(bf16[4000,768]{1,0:T(8,128)(2,1)} %all-gather.5.cloned.1.call-done, bf16[4000,768]{1,0:T(8,128)(2,1)} %get-tuple-element.181), kind=kOutput, calls=%fused_computation.79 | convolution fusion | flops 4719181824 | bytes 13467648 | tf_op jit(solution)/shard_map/dot_general | solution.py:202
  584.0 10.0 %convolution_convert_fusion.4 = bf16[768,768]{0,1:T(8,128)(2,1)} fusion(bf16[4000,768]{1,0:T(8,128)(2,1)} %all-gather.3.cloned.1.call-done, bf16[4000,768]{1,0:T(8,128)(2,1)} %copy-done.38), kind=kOutput, calls=%fused_computation.80 | convolution fusion | flops 4719181824 | bytes 13467648 | tf_op jit(solution)/shard_map/dot_general | solution.py:206
  594.0 20.4 %reduce-scatter.9.cloned.1.call-done = bf16[768,576]{0,1:T(8,128)(2,1)} async-done(((bf16[768,2304]{0,1:T(8,128)(2,1)}), bf16[768,576]{0,1:T(8,128)(2,1)}) %reduce-scatter.9.cloned.1.call-update) | async-done | bytes 884752 | tf_op jit(solution)/shard_map/reduce_scatter | solution.py:288
  650.0 10.1 %multiply_reduce_fusion.4 = (f32[768]{0:T(1024)S(1)}, f32[1000]{0:T(1024)}, f32[1000]{0:T(1024)}, f32[768]{0:T(1024)S(1)}, f32[1000,768]{1,0:T(8,128)}) fusion(f32[1000]{0:T(1024)} %rsqrt.21, f32[1000]{0:T(1024)} %div.123, bf16[5,200,768]{2,1,0:T(8,128)(2,1)} %param.33, f32[768]{0:T(1024)S(1)} %copy-done.28, bf16[1000,2304]{0,1:T(8,128)(2,1)} %convert_element_type.177, ...), kind=kOutput, calls=%fused_computation.45 | convolution fusion | flops 3548924416 | bytes 14316160 | tf_op jit(solution)/shard_map/dot_general | solution.py:262
  665.5 59.9 %while.22 = (s32[]{:T(128)}, f32[732,12]{0,1:T(8,128)}, s32[8,25,200]{2,1,0:T(8,128)}, f32[8,12,25,200]{3,2,0,1:T(8,128)}, s32[]{:T(128)}, /*index=5*/s32[]{:T(128)}) while((s32[]{:T(128)}, f32[732,12]{0,1:T(8,128)}, s32[8,25,200]{2,1,0:T(8,128)}, f32[8,12,25,200]{3,2,0,1:T(8,128)}, s32[]{:T(128)}, /*index=5*/s32[]{:T(128)}) %tuple.116), condition=%wide.region_39.40_spmd.clone, body=%wide.region_38.39_spmd.clone.sunk | while | flops 530717568 | bytes 850367 | solution.py:97
  739.4 118.5 %all-reduce.4.cloned.1.call-done = (f32[32]{0:T(128)}, f32[10,768]{1,0:T(8,128)}, f32[3072]{0:T(1024)}, f32[732,12]{0,1:T(8,128)}) async-done(((f32[32]{0:T(128)}, f32[10,768]{1,0:T(8,128)}, f32[3072]{0:T(1024)}, f32[732,12]{0,1:T(8,128)}), (f32[32]{0:T(128)}, f32[10,768]{1,0:T(8,128)}, f32[3072]{0:T(1024)}, f32[732,12]{0,1:T(8,128)})) %all-reduce.4.cloned.1.call-update) | async-done | bytes 78288
  (226 shorter events, 333.4 us)
Async XLA Ops:
  7.2 95.4 %copy-start = (bf16[768,2304]{1,0:T(8,128)(2,1)S(1)}, bf16[768,2304]{1,0:T(8,128)(2,1)}, u32[]{:S(2)}) copy-start(bf16[768,2304]{1,0:T(8,128)(2,1)} %param.37) | copy-start | bytes 10616836
  7.2 228.9 %all-gather.3.cloned.1.call-start = ((), (), s32[]{:S(2)}) async-start(), calls=%async_computation.5 | async-start | bytes 7680000 | tf_op jit(solution)/shard_map/all_gather | solution.py:179
  187.7 95.5 %all-gather.5.cloned.1.call-start = ((), (), s32[]{:S(2)}) async-start(), calls=%async_computation.7 | async-start | bytes 7680000 | tf_op jit(solution)/shard_map/all_gather | solution.py:200
  193.4 210.7 %reduce-scatter.7.cloned.1.call-start = ((), (), s32[]{:S(2)}) async-start(), calls=%async_computation.8 | async-start | bytes 15360000 | tf_op jit(solution)/shard_map/reduce_scatter | solution.py:214
  283.2 15.1 %copy-start.37 = (bf16[768,768]{1,0:T(8,128)(2,1)S(1)}, bf16[768,768]{1,0:T(8,128)(2,1)}, u32[]{:S(2)}) copy-start(bf16[768,768]{1,0:T(8,128)(2,1)} %param.39) | copy-start | bytes 3538948
  306.3 158.1 %reduce-scatter.5.cloned.1.call-start = ((), (), s32[]{:S(2)}) async-start(), calls=%async_computation.6 | async-start | bytes 7680000 | tf_op jit(solution)/shard_map/reduce_scatter | solution.py:184
  319.4 274.5 %reduce-scatter.11.cloned.1.call-start = ((), (), s32[]{:S(2)}) async-start(), calls=%async_computation.10 | async-start | bytes 1474560 | tf_op jit(solution)/shard_map/reduce_scatter | solution.py:291
  323.3 141.2 %copy-start.23 = (f32[768]{0:T(1024)S(1)}, f32[768]{0:T(1024)}, u32[]{:S(2)}) copy-start(f32[768]{0:T(1024)} %get-tuple-element.105) | copy-start | bytes 9220
  323.3 141.2 %copy-start.25 = (f32[1000]{0:T(1024)S(1)}, f32[1000]{0:T(1024)}, u32[]{:S(2)}) copy-start(f32[1000]{0:T(1024)} %copy-done.24) | copy-start | bytes 12004
  464.4 10.0 %copy-start.32 = (f32[768]{0:T(1024)S(1)}, f32[768]{0:T(1024)}, u32[]{:S(2)}) copy-start(f32[768]{0:T(1024)} %get-tuple-element.111) | copy-start | bytes 9220
  483.5 130.9 %reduce-scatter.9.cloned.1.call-start = ((), (), s32[]{:S(2)}) async-start(), calls=%async_computation.9 | async-start | bytes 4423680 | tf_op jit(solution)/shard_map/reduce_scatter | solution.py:288
  495.5 13.1 %copy-start.10 = (f32[5,12,200]{2,1,0:T(8,128)S(1)}, f32[5,12,200]{2,1,0:T(8,128)}, u32[]{:S(2)}) copy-start(f32[5,12,200]{2,1,0:T(8,128)} %copy-done.9) | copy-start | bytes 144004
  508.6 19.9 %slice-start = ((s8[12288000]{0:T(1024)(128)(4,1)}), s8[4194304]{0:T(1024)(128)(4,1)S(1)}, s32[]{:S(2)}) async-start(s8[12288000]{0:T(1024)(128)(4,1)} %bitcast.123), calls=%async_computation.12 | async-start | bytes 8388608
  508.6 19.9 %slice-start.1 = ((s8[12288000]{0:T(1024)(128)(4,1)}), s8[4194304]{0:T(1024)(128)(4,1)S(1)}, s32[]{:S(2)}) async-start(s8[12288000]{0:T(1024)(128)(4,1)} %bitcast.123), calls=%async_computation.13 | async-start | bytes 8388608
  623.6 101.7 %all-to-all-start = ((bf16[8,96,2304]{2,1,0:T(8,128)(2,1)}), bf16[8,96,2304]{2,1,0:T(8,128)(2,1)}, u32[]{:S(2)}, u32[]{:S(2)}) async-start(bf16[8,96,2304]{2,1,0:T(8,128)(2,1)} %bitcast.127), calls=%async_computation.4 | async-start | bytes 7077888 | tf_op jit(solution)/shard_map/all_to_all | solution.py:30
  629.2 228.7 %all-reduce.4.cloned.1.call-start = ((), (), s32[]{:S(2)}) async-start(), calls=%async_computation.11 | async-start | bytes 222208
  632.8 17.2 %copy-start.26 = (f32[3072]{0:T(1024)}, f32[3072]{0:T(1024)S(1)}, u32[]{:S(2)}) copy-start(f32[3072]{0:T(1024)S(1)} %dynamic_update_slice.7) | copy-start | bytes 36868
  733.5 132.5 %copy-start.29 = (f32[3072]{0:T(1024)S(1)}, f32[3072]{0:T(1024)}, u32[]{:S(2)}) copy-start(f32[3072]{0:T(1024)} %param.42) | copy-start | bytes 36868
  865.9 8.9 %copy-start.7 = (f32[96,2304]{1,0:T(8,128)S(1)}, f32[96,2304]{1,0:T(8,128)}, u32[]{:S(2)}) copy-start(f32[96,2304]{1,0:T(8,128)} %copy-done.6) | copy-start | bytes 2654212
  866.0 8.9 %copy-start.13 = (f32[96,768]{1,0:T(8,128)S(1)}, f32[96,768]{1,0:T(8,128)}, u32[]{:S(2)}) copy-start(f32[96,768]{1,0:T(8,128)} %param.53) | copy-start | bytes 884740
  866.0 8.9 %copy-start.14 = (f32[96,768]{1,0:T(8,128)S(1)}, f32[96,768]{1,0:T(8,128)}, u32[]{:S(2)}) copy-start(f32[96,768]{1,0:T(8,128)} %param.55) | copy-start | bytes 884740
  866.0 8.9 %copy-start.15 = (f32[96,768]{1,0:T(8,128)S(1)}, f32[96,768]{1,0:T(8,128)}, u32[]{:S(2)}) copy-start(f32[96,768]{1,0:T(8,128)} %param.54) | copy-start | bytes 884740
  866.0 8.9 %copy-start.16 = (f32[96,768]{1,0:T(8,128)S(1)}, f32[96,768]{1,0:T(8,128)}, u32[]{:S(2)}) copy-start(f32[96,768]{1,0:T(8,128)} %param.50) | copy-start | bytes 884740
  866.0 8.9 %copy-start.17 = (f32[96,768]{1,0:T(8,128)S(1)}, f32[96,768]{1,0:T(8,128)}, u32[]{:S(2)}) copy-start(f32[96,768]{1,0:T(8,128)} %param.52) | copy-start | bytes 884740
  (26 other events, 110.7 us)
Sparse Core Ops, SparseCore 0:
  187.8 48.2 all-gather.2
  237.7 45.5 all-gather.4
  306.4 97.6 reduce-scatter.6
  406.5 57.8 reduce-scatter.4
  483.6 25.6 reduce-scatter.10
  573.9 40.3 reduce-scatter.8
  733.6 124.2 all-reduce.3
